TPU v7x, 32 devices: a whole 2x2x4 slice. The times are simulated.
32 devices in a mesh: chan: 8 (over z, y), tm: 4 (over x, core).
Axes of the slice: x: 2, y: 2, z: 4, core: 2. Of those that a mesh axis runs over, the one named last changes fastest.
Arguments:
- record: bfloat16 [96, 2048], P('chan', 'tm'), may hold values from -6 to 6
- fir: float32 [96, 65], P('chan'), may hold values from -0.75 to 0.75
Outputs:
- xcorr: float32 [4, 96, 96, 256], P('tm', 'chan')
All inputs are finite; a program needn't handle non-finite values.
Results may differ from a plain program's by a relative error of at most 0.004.
Values may be sent and summed in bfloat16 or wider, within the bound.
A program may use at most 64 MiB of HBM per device.

v0:
```python
import math
import jax
import jax.numpy as jnp
from jax import lax
from jax.sharding import PartitionSpec as P

GROUP = 512
MAXLAG = 128


def extended_2(block, sides, width):
    for axis, dim in sides:
        count = lax.axis_size(axis)
        forward = [(i, i + 1) for i in range(count - 1)]
        backward = [(target, source) for source, target in forward]
        low = lax.ppermute(
            lax.slice_in_dim(block, block.shape[dim] - width, None, axis=dim), axis, forward
        )
        high = lax.ppermute(lax.slice_in_dim(block, 0, width, axis=dim), axis, backward)
        block = jnp.concatenate([low, block, high], axis=dim)
    return block


def whiten(widened_raw, fir, length):
    widened = widened_raw.astype(jnp.float32)
    running = jnp.zeros((widened.shape[0], length), jnp.float32)
    for k in range(fir.shape[1]):
        running = running + fir[:, k : k + 1] * widened[:, k : k + length]
    return running


def local(record, fir):
    ch_dev = record.shape[0]
    local_len = record.shape[1]
    half_width = (fir.shape[1] - 1) // 2
    lag_count = 2 * MAXLAG
    span = GROUP + lag_count
    factor = 1.0 / math.sqrt(GROUP)
    raw_ext = extended_2(record, (("tm", 1),), half_width)
    whitened = whiten(raw_ext, fir, local_len).astype(jnp.bfloat16)
    extended = extended_2(whitened, (("tm", 1),), MAXLAG)
    c = 0
    segment = extended[:, c * GROUP + MAXLAG : c * GROUP + MAXLAG + GROUP]
    padded = jnp.concatenate([segment, jnp.zeros((ch_dev, lag_count + 1), jnp.bfloat16)], axis=1)
    tiled = jnp.tile(padded, (1, lag_count))[:, : lag_count * span]
    expanded = [tiled.reshape(ch_dev, lag_count, span)]
    c = 0
    window = lax.all_gather(extended, "chan", axis=0, tiled=True)
    blocks = [
        jnp.einsum("amu,ju->ajm", expanded[c], window, preferred_element_type=jnp.float32) * factor
    ]
    return jnp.stack(blocks)


def solution(mesh):
    in_specs = (P("chan", "tm"), P("chan", None))
    out_specs = P("tm", "chan", None, None)
    return jax.shard_map(local, mesh=mesh, in_specs=in_specs, out_specs=out_specs, check_vma=False)
```

profile of v0, /device:TPU:6, one launch (start us, length us, event | category | flops | bytes accessed | tf_op | source)
XLA Modules:
  0.0 80.0 jit_solution(231138366995109417)
XLA Ops:
  0.0 0.8 fusion.74
  0.8 1.9 %collective-permute-start = (bf16[12,32]{1,0:T(8,128)(2,1)S(1)}, bf16[12,32]{1,0:T(8,128)(2,1)S(1)}, u32[]{:S(2)}, u32[]{:S(2)}) collective-permute-start(bf16[12,32]{1,0:T(8,128)(2,1)S(1)} %get-tuple-element.72), channel_id=1, source_target_pairs={{0,1},{1,2},{2,3},{4,5},{5,6},{6,7},{8,9},{9,10},{10,11},{12,13},{... | collective-permute-start | bytes 2312 | tf_op jit(solution)/shard_map/ppermute | solution.py:16
  2.7 3.6 %collective-permute-start.1 = (bf16[12,32]{1,0:T(8,128)(2,1)S(1)}, bf16[12,32]{1,0:T(8,128)(2,1)S(1)}, u32[]{:S(2)}, u32[]{:S(2)}) collective-permute-start(bf16[12,32]{1,0:T(8,128)(2,1)S(1)} %get-tuple-element.73), channel_id=1, source_target_pairs={{1,0},{2,1},{3,2},{5,4},{6,5},{7,6},{9,8},{10,9},{11,10},{13,12},{... | collective-permute-start | bytes 2312 | tf_op jit(solution)/shard_map/ppermute | solution.py:19
  6.3 1.9 %slice_reduce_fusion.64 = (f32[12]{0:T(128)S(1)}, f32[12]{0:T(128)S(1)}, f32[12]{0:T(128)S(1)}, f32[12]{0:T(128)S(1)}, f32[12]{0:T(128)S(1)}, /*index=5*/f32[12]...) fusion(f32[12,65]{1,0:T(8,128)} %param.3), kind=kLoop, calls=%fused_computation.200 | loop fusion | bytes 1824 | tf_op jit(solution)/shard_map/slice | solution.py:28
  8.3 1.9 %slice_reduce_fusion.63 = (f32[12]{0:T(128)S(1)}, f32[12]{0:T(128)S(1)}, f32[12]{0:T(128)S(1)}, f32[12]{0:T(128)S(1)}, f32[12]{0:T(128)S(1)}, /*index=5*/f32[12]...) fusion(f32[12,65]{1,0:T(8,128)} %param.3), kind=kLoop, calls=%fused_computation.199 | loop fusion | bytes 1824 | tf_op jit(solution)/shard_map/slice | solution.py:28
  10.2 1.9 %slice_reduce_fusion.62 = (f32[12]{0:T(128)S(1)}, f32[12]{0:T(128)S(1)}, f32[12]{0:T(128)S(1)}, f32[12]{0:T(128)S(1)}, f32[12]{0:T(128)S(1)}, /*index=5*/f32[12]...) fusion(f32[12,65]{1,0:T(8,128)} %param.3), kind=kLoop, calls=%fused_computation.198 | loop fusion | bytes 1824 | tf_op jit(solution)/shard_map/slice | solution.py:28
  12.1 1.3 %slice_reduce_fusion.61 = (f32[12]{0:T(128)S(1)}, f32[12]{0:T(128)S(1)}, f32[12]{0:T(128)S(1)}, f32[12]{0:T(128)S(1)}, f32[12]{0:T(128)S(1)}, /*index=5*/f32[12]{0:T(128)S(1)}, f32[12]{0:T(128)S(1)}, f32[12]{0:T(128)S(1)}) fusion(f32[12,65]{1,0:T(8,128)} %param.3), kind=kLoop, calls=%fused_computation.197 | loop fusion | bytes 768 | tf_op jit(solution)/shard_map/slice | solution.py:28
  13.4 0.0 collective-permute-done
  13.5 0.0 collective-permute-done.1
  13.5 0.8 maximum_convert_fusion
  14.3 0.8 fusion.9
  15.1 1.9 %collective-permute-start.2 = (bf16[12,128]{1,0:T(8,128)(2,1)S(1)}, bf16[12,128]{1,0:T(8,128)(2,1)S(1)}, u32[]{:S(2)}, u32[]{:S(2)}) collective-permute-start(bf16[12,128]{1,0:T(8,128)(2,1)S(1)} %get-tuple-element.70), channel_id=1, source_target_pairs={{0,1},{1,2},{2,3},{4,5},{5,6},{6,7},{8,9},{9,10},{10,11},{12,13},{... | collective-permute-start | bytes 9224 | tf_op jit(solution)/shard_map/ppermute | solution.py:16
  17.0 3.6 %collective-permute-start.3 = (bf16[12,128]{1,0:T(8,128)(2,1)S(1)}, bf16[12,128]{1,0:T(8,128)(2,1)S(1)}, u32[]{:S(2)}, u32[]{:S(2)}) collective-permute-start(bf16[12,128]{1,0:T(8,128)(2,1)S(1)} %get-tuple-element.71), channel_id=1, source_target_pairs={{1,0},{2,1},{3,2},{5,4},{6,5},{7,6},{9,8},{10,9},{11,10},{13,12},{... | collective-permute-start | bytes 9224 | tf_op jit(solution)/shard_map/ppermute | solution.py:19
  20.7 2.9 %tile.4 = bf16[12,256,769]{2,1,0:T(8,128)(2,1)} broadcast(bf16[12,769]{1,0:T(8,128)(2,1)S(1)} %concatenate.11), dimensions={0,2} | broadcast | bytes 4743192 | tf_op jit(solution)/shard_map/tile | solution.py:45
  23.5 13.6 %tile.10 = bf16[12,196864]{1,0:T(8,128)(2,1)} reshape(bf16[12,256,769]{2,1,0:T(8,128)(2,1)} %tile.4) | data formatting | bytes 9449472 | tf_op jit(solution)/shard_map/tile | solution.py:45
  37.1 0.0 slice-start
  37.1 2.8 %slice-done = bf16[12,196608]{1,0:T(8,128)(2,1)S(1)} async-done(((bf16[12,196864]{1,0:T(8,128)(2,1)}), bf16[12,196608]{1,0:T(8,128)(2,1)S(1)}, s32[]{:S(2)}) %slice-start) | async-done | bytes 4718616 | tf_op jit(solution)/shard_map/slice | solution.py:45
  39.9 4.1 %copy.3 = bf16[2,8,256,768]{3,2,1,0:T(8,128)(2,1)} copy(bf16[2,8,256,768]{3,1,2,0:T(8,128)(2,1)S(1)} %bitcast.10) | data formatting | bytes 12582912
  44.0 0.0 collective-permute-done.2
  44.0 0.0 collective-permute-done.3
  44.0 31.0 %all-gather = bf16[8,12,768]{2,1,0:T(8,128)(2,1)S(1)} all-gather(bf16[1,12,768]{2,1,0:T(8,128)(2,1)S(1)} %maximum_bitcast_fusion), channel_id=1, replica_groups=mesh['chan'=8,'tm'=4] {'chan'}, dimensions={0}, use_global_device_ids=true | all-gather | bytes 165888 | tf_op jit(solution)/shard_map/all_gather | solution.py:48
  75.1 4.9 %fusion.5 = f32[1,12,96,256]{3,2,1,0:T(8,128)} fusion(bf16[96,768,1]{1,0,2:T(8,128)(2,1)S(1)} %reshape.10, bf16[16,256,768]{2,1,0:T(8,128)(2,1)} %bitcast.11), kind=kOutput, calls=%fused_computation.3 | convolution fusion | flops 453279744 | bytes 6045696 | tf_op jit(solution)/shard_map/amu,ju->ajm/dot_general | solution.py:50
  (4 shorter events, 0.1 us)
Async XLA Ops:
  0.8 12.7 %collective-permute-start = (bf16[12,32]{1,0:T(8,128)(2,1)S(1)}, bf16[12,32]{1,0:T(8,128)(2,1)S(1)}, u32[]{:S(2)}, u32[]{:S(2)}) collective-permute-start(bf16[12,32]{1,0:T(8,128)(2,1)S(1)} %get-tuple-element.72), channel_id=1, source_target_pairs={{0,1},{1,2},{2,3},{4,5},{5,6},{6,7},{8,9},{9,10},{10,11},{12,13},{... | collective-permute-start | bytes 2312 | tf_op jit(solution)/shard_map/ppermute | solution.py:16
  2.7 10.8 %collective-permute-start.1 = (bf16[12,32]{1,0:T(8,128)(2,1)S(1)}, bf16[12,32]{1,0:T(8,128)(2,1)S(1)}, u32[]{:S(2)}, u32[]{:S(2)}) collective-permute-start(bf16[12,32]{1,0:T(8,128)(2,1)S(1)} %get-tuple-element.73), channel_id=1, source_target_pairs={{1,0},{2,1},{3,2},{5,4},{6,5},{7,6},{9,8},{10,9},{11,10},{13,12},{... | collective-permute-start | bytes 2312 | tf_op jit(solution)/shard_map/ppermute | solution.py:19
  15.1 28.9 %collective-permute-start.2 = (bf16[12,128]{1,0:T(8,128)(2,1)S(1)}, bf16[12,128]{1,0:T(8,128)(2,1)S(1)}, u32[]{:S(2)}, u32[]{:S(2)}) collective-permute-start(bf16[12,128]{1,0:T(8,128)(2,1)S(1)} %get-tuple-element.70), channel_id=1, source_target_pairs={{0,1},{1,2},{2,3},{4,5},{5,6},{6,7},{8,9},{9,10},{10,11},{12,13},{... | collective-permute-start | bytes 9224 | tf_op jit(solution)/shard_map/ppermute | solution.py:16
  17.0 27.0 %collective-permute-start.3 = (bf16[12,128]{1,0:T(8,128)(2,1)S(1)}, bf16[12,128]{1,0:T(8,128)(2,1)S(1)}, u32[]{:S(2)}, u32[]{:S(2)}) collective-permute-start(bf16[12,128]{1,0:T(8,128)(2,1)S(1)} %get-tuple-element.71), channel_id=1, source_target_pairs={{1,0},{2,1},{3,2},{5,4},{6,5},{7,6},{9,8},{10,9},{11,10},{13,12},{... | collective-permute-start | bytes 9224 | tf_op jit(solution)/shard_map/ppermute | solution.py:19
  37.1 2.8 %slice-start = ((bf16[12,196864]{1,0:T(8,128)(2,1)}), bf16[12,196608]{1,0:T(8,128)(2,1)S(1)}, s32[]{:S(2)}) async-start(bf16[12,196864]{1,0:T(8,128)(2,1)} %tile.10), calls=%async_computation | async-start | bytes 12582912 | tf_op jit(solution)/shard_map/slice | solution.py:45
where the time goes:
time: 80.6 us; the launch traced here: 80 us
  local copies, waits for them, and re-layouts  31.2 us (39%)
  blocking collectives  31 us (38%)
  starting transfers between devices  11.1 us (14%)
  matrix products  4.89 us (6%)
  other arithmetic  1.59 us (2%)
    all_gather x1, blocking collectives, local(): window = lax.all_gather(extended, 'chan', axis=0, tiled=True)  31 us
    another operation x2, local copies, waits for them, and re-layouts, local(): tiled = jnp.tile(padded, (1, lag_count))[:, :lag_count * span]  16.5 us
    ppermute x2, starting transfers between devices, extended_2(): lax.ppermute(lax.slice_in_dim(block, 0, width, axis=dim), axis, backward)  7.28 us
    slice x4, local copies, waits for them, and re-layouts, whiten(): running = running + fir[:, k:k + 1] * widened[:, k:k + length]  7.1 us
    dot_general x1, matrix products, local(): jnp.einsum('amu,ju->ajm', expanded[c], window, preferred_element_type=jnp...  4.89 us
    unnamed x2, local copies, waits for them, and re-layouts  4.09 us
    ppermute x2, starting transfers between devices, extended_2(): lax.ppermute(lax.slice_in_dim(block, block.shape[dim] - width, None, axis...  3.83 us
    slice x2, local copies, waits for them, and re-layouts, local(): tiled = jnp.tile(padded, (1, lag_count))[:, :lag_count * span]  2.78 us
  transfers between devices with their start and end apart: 4, of which 0 were waited for; matrix products, arithmetic and copies ran while one was open for 35% of the time, Pallas kernels for 0%

commit v1 on v0

--- a/solution.py
+++ b/solution.py
@@ -45,7 +45,12 @@
     tiled = jnp.tile(padded, (1, lag_count))[:, : lag_count * span]
     expanded = [tiled.reshape(ch_dev, lag_count, span)]
     c = 0
-    window = lax.all_gather(extended, "chan", axis=0, tiled=True)
+    ring = [extended]
+    for hop in range(7):
+        ring.append(lax.ppermute(ring[-1], "chan", [(dev, (dev + 1) % 8) for dev in range(8)]))
+    window = jnp.roll(
+        jnp.concatenate(ring[::-1], axis=0), (lax.axis_index("chan") + 1) * ring[0].shape[0], axis=0
+    )
     blocks = [
         jnp.einsum("amu,ju->ajm", expanded[c], window, preferred_element_type=jnp.float32) * factor
     ]

time: 80.6 us -> 91.8 us (1.14)
  the two profiles are of different devices: /device:TPU:6 before, /device:TPU:0 now
where the time goes in v1:
time: 91.8 us; the launch traced here: 91.1 us
  waiting for transfers between devices  40.6 us (44%)
  local copies, waits for them, and re-layouts  32.3 us (35%)
  starting transfers between devices  11.6 us (13%)
  matrix products  4.9 us (5%)
  other arithmetic  1.59 us (2%)
    ppermute x7, waiting for transfers between devices, local(): lax.ppermute(ring[-1], 'chan', [(dev, (dev + 1) % 8) for dev in range(8)])  37.6 us
    another operation x2, local copies, waits for them, and re-layouts, local(): tiled = jnp.tile(padded, (1, lag_count))[:, :lag_count * span]  16.5 us
    ppermute x2, starting transfers between devices, extended_2(): lax.ppermute(lax.slice_in_dim(block, block.shape[dim] - width, None, axis...  7.48 us
    slice x4, local copies, waits for them, and re-layouts, whiten(): running = running + fir[:, k:k + 1] * widened[:, k:k + length]  7.1 us
    dot_general x1, matrix products, local(): jnp.einsum('amu,ju->ajm', expanded[c], window, preferred_element_type=jnp...  4.9 us
    unnamed x1, local copies, waits for them, and re-layouts  4.05 us
    ppermute x2, waiting for transfers between devices, extended_2(): lax.ppermute(lax.slice_in_dim(block, 0, width, axis=dim), axis, backward)  2.99 us
    slice x2, local copies, waits for them, and re-layouts, local(): tiled = jnp.tile(padded, (1, lag_count))[:, :lag_count * span]  2.78 us
  transfers between devices with their start and end apart: 11, of which 7 were waited for; matrix products, arithmetic and copies ran while one was open for 30% of the time, Pallas kernels for 0%

profile of v1, /device:TPU:0, one launch (start us, length us, event | category | flops | bytes accessed | tf_op | source)
XLA Modules:
  0.0 91.1 jit_solution(11939581738660626679)
XLA Ops:
  0.0 0.8 fusion.77
  0.8 2.3 %collective-permute-start = (bf16[12,32]{1,0:T(8,128)(2,1)S(1)}, bf16[12,32]{1,0:T(8,128)(2,1)S(1)}, u32[]{:S(2)}, u32[]{:S(2)}) collective-permute-start(bf16[12,32]{1,0:T(8,128)(2,1)S(1)} %get-tuple-element.72), channel_id=1, source_target_pairs={{0,1},{1,2},{2,3},{4,5},{5,6},{6,7},{8,9},{9,10},{10,11},{12,13},{... | collective-permute-start | bytes 2312 | tf_op jit(solution)/shard_map/ppermute | solution.py:16
  3.1 1.3 %collective-permute-start.1 = (bf16[12,32]{1,0:T(8,128)(2,1)S(1)}, bf16[12,32]{1,0:T(8,128)(2,1)S(1)}, u32[]{:S(2)}, u32[]{:S(2)}) collective-permute-start(bf16[12,32]{1,0:T(8,128)(2,1)S(1)} %get-tuple-element.73), channel_id=1, source_target_pairs={{1,0},{2,1},{3,2},{5,4},{6,5},{7,6},{9,8},{10,9},{11,10},{13,12},{... | collective-permute-start | bytes 2312 | tf_op jit(solution)/shard_map/ppermute | solution.py:19
  4.4 1.9 %slice_reduce_fusion.64 = (f32[12]{0:T(128)S(1)}, f32[12]{0:T(128)S(1)}, f32[12]{0:T(128)S(1)}, f32[12]{0:T(128)S(1)}, f32[12]{0:T(128)S(1)}, /*index=5*/f32[12]...) fusion(f32[12,65]{1,0:T(8,128)} %param.3), kind=kLoop, calls=%fused_computation.202 | loop fusion | bytes 1824 | tf_op jit(solution)/shard_map/slice | solution.py:28
  6.4 1.9 %slice_reduce_fusion.63 = (f32[12]{0:T(128)S(1)}, f32[12]{0:T(128)S(1)}, f32[12]{0:T(128)S(1)}, f32[12]{0:T(128)S(1)}, f32[12]{0:T(128)S(1)}, /*index=5*/f32[12]...) fusion(f32[12,65]{1,0:T(8,128)} %param.3), kind=kLoop, calls=%fused_computation.201 | loop fusion | bytes 1824 | tf_op jit(solution)/shard_map/slice | solution.py:28
  8.3 1.9 %slice_reduce_fusion.62 = (f32[12]{0:T(128)S(1)}, f32[12]{0:T(128)S(1)}, f32[12]{0:T(128)S(1)}, f32[12]{0:T(128)S(1)}, f32[12]{0:T(128)S(1)}, /*index=5*/f32[12]...) fusion(f32[12,65]{1,0:T(8,128)} %param.3), kind=kLoop, calls=%fused_computation.200 | loop fusion | bytes 1824 | tf_op jit(solution)/shard_map/slice | solution.py:28
  10.2 1.3 %slice_reduce_fusion.61 = (f32[12]{0:T(128)S(1)}, f32[12]{0:T(128)S(1)}, f32[12]{0:T(128)S(1)}, f32[12]{0:T(128)S(1)}, f32[12]{0:T(128)S(1)}, /*index=5*/f32[12]{0:T(128)S(1)}, f32[12]{0:T(128)S(1)}, f32[12]{0:T(128)S(1)}) fusion(f32[12,65]{1,0:T(8,128)} %param.3), kind=kLoop, calls=%fused_computation.199 | loop fusion | bytes 768 | tf_op jit(solution)/shard_map/slice | solution.py:28
  11.5 0.0 collective-permute-done
  11.5 0.0 collective-permute-done.1
  11.6 0.8 maximum_convert_fusion
  12.3 0.8 fusion.11
  13.2 5.1 %collective-permute-start.2 = (bf16[12,128]{1,0:T(8,128)(2,1)S(1)}, bf16[12,128]{1,0:T(8,128)(2,1)S(1)}, u32[]{:S(2)}, u32[]{:S(2)}) collective-permute-start(bf16[12,128]{1,0:T(8,128)(2,1)S(1)} %get-tuple-element.70), channel_id=1, source_target_pairs={{0,1},{1,2},{2,3},{4,5},{5,6},{6,7},{8,9},{9,10},{10,11},{12,13},{... | collective-permute-start | bytes 9224 | tf_op jit(solution)/shard_map/ppermute | solution.py:16
  18.3 1.3 %collective-permute-start.3 = (bf16[12,128]{1,0:T(8,128)(2,1)S(1)}, bf16[12,128]{1,0:T(8,128)(2,1)S(1)}, u32[]{:S(2)}, u32[]{:S(2)}) collective-permute-start(bf16[12,128]{1,0:T(8,128)(2,1)S(1)} %get-tuple-element.71), channel_id=1, source_target_pairs={{1,0},{2,1},{3,2},{5,4},{6,5},{7,6},{9,8},{10,9},{11,10},{13,12},{... | collective-permute-start | bytes 9224 | tf_op jit(solution)/shard_map/ppermute | solution.py:19
  19.6 0.0 collective-permute-done.2
  19.6 3.0 %collective-permute-done.3 = bf16[12,128]{1,0:T(8,128)(2,1)S(1)} collective-permute-done((bf16[12,128]{1,0:T(8,128)(2,1)S(1)}, bf16[12,128]{1,0:T(8,128)(2,1)S(1)}, u32[]{:S(2)}, u32[]{:S(2)}) %collective-permute-start.3) | collective-permute-done | bytes 3104 | tf_op jit(solution)/shard_map/ppermute | solution.py:19
  22.6 1.5 %collective-permute-start.4 = (bf16[12,768]{1,0:T(8,128)(2,1)S(1)}, bf16[12,768]{1,0:T(8,128)(2,1)S(1)}, u32[]{:S(2)}, u32[]{:S(2)}) collective-permute-start(bf16[12,768]{1,0:T(8,128)(2,1)S(1)} %pad_maximum_fusion), channel_id=1, source_target_pairs={{0,4},{4,8},{8,12},{12,16},{16,20},{20,24},{24,28},{28,0},{1,5},{5... | collective-permute-start | bytes 55304 | tf_op jit(solution)/shard_map/ppermute | solution.py:50
  24.1 5.0 %collective-permute-done.4 = bf16[12,768]{1,0:T(8,128)(2,1)S(1)} collective-permute-done((bf16[12,768]{1,0:T(8,128)(2,1)S(1)}, bf16[12,768]{1,0:T(8,128)(2,1)S(1)}, u32[]{:S(2)}, u32[]{:S(2)}) %collective-permute-start.4) | collective-permute-done | bytes 18464 | tf_op jit(solution)/shard_map/ppermute | solution.py:50
  29.1 6.5 %collective-permute-done.5 = bf16[12,768]{1,0:T(8,128)(2,1)S(1)} collective-permute-done((bf16[12,768]{1,0:T(8,128)(2,1)S(1)}, bf16[12,768]{1,0:T(8,128)(2,1)S(1)}, u32[]{:S(2)}, u32[]{:S(2)}) %collective-permute-start.5) | collective-permute-done | bytes 18464 | tf_op jit(solution)/shard_map/ppermute | solution.py:50
  35.7 0.0 collective-permute-start.6
  35.7 6.5 %collective-permute-done.6 = bf16[12,768]{1,0:T(8,128)(2,1)S(1)} collective-permute-done((bf16[12,768]{1,0:T(8,128)(2,1)S(1)}, bf16[12,768]{1,0:T(8,128)(2,1)S(1)}, u32[]{:S(2)}, u32[]{:S(2)}) %collective-permute-start.6) | collective-permute-done | bytes 18464 | tf_op jit(solution)/shard_map/ppermute | solution.py:50
  42.2 6.5 %collective-permute-done.7 = bf16[12,768]{1,0:T(8,128)(2,1)S(1)} collective-permute-done((bf16[12,768]{1,0:T(8,128)(2,1)S(1)}, bf16[12,768]{1,0:T(8,128)(2,1)S(1)}, u32[]{:S(2)}, u32[]{:S(2)}) %collective-permute-start.7) | collective-permute-done | bytes 18464 | tf_op jit(solution)/shard_map/ppermute | solution.py:50
  48.7 0.0 collective-permute-start.8
  48.7 6.5 %collective-permute-done.8 = bf16[12,768]{1,0:T(8,128)(2,1)S(1)} collective-permute-done((bf16[12,768]{1,0:T(8,128)(2,1)S(1)}, bf16[12,768]{1,0:T(8,128)(2,1)S(1)}, u32[]{:S(2)}, u32[]{:S(2)}) %collective-permute-start.8) | collective-permute-done | bytes 18464 | tf_op jit(solution)/shard_map/ppermute | solution.py:50
  55.2 6.5 %collective-permute-done.9 = bf16[12,768]{1,0:T(8,128)(2,1)S(1)} collective-permute-done((bf16[12,768]{1,0:T(8,128)(2,1)S(1)}, bf16[12,768]{1,0:T(8,128)(2,1)S(1)}, u32[]{:S(2)}, u32[]{:S(2)}) %collective-permute-start.9) | collective-permute-done | bytes 18464 | tf_op jit(solution)/shard_map/ppermute | solution.py:50
  61.8 0.0 collective-permute-start.10
  61.8 2.9 %tile.4 = bf16[12,256,769]{2,1,0:T(8,128)(2,1)} broadcast(bf16[12,769]{1,0:T(8,128)(2,1)S(1)} %concatenate.18), dimensions={0,2} | broadcast | bytes 4743192 | tf_op jit(solution)/shard_map/tile | solution.py:45
  64.6 13.6 %tile.10 = bf16[12,196864]{1,0:T(8,128)(2,1)} reshape(bf16[12,256,769]{2,1,0:T(8,128)(2,1)} %tile.4) | data formatting | bytes 9449472 | tf_op jit(solution)/shard_map/tile | solution.py:45
  78.2 2.8 %slice-done = bf16[12,196608]{1,0:T(8,128)(2,1)S(1)} async-done(((bf16[12,196864]{1,0:T(8,128)(2,1)}), bf16[12,196608]{1,0:T(8,128)(2,1)S(1)}, s32[]{:S(2)}) %slice-start) | async-done | bytes 4718616 | tf_op jit(solution)/shard_map/slice | solution.py:45
  81.0 4.1 %copy.3 = bf16[2,8,256,768]{3,2,1,0:T(8,128)(2,1)} copy(bf16[2,8,256,768]{3,1,2,0:T(8,128)(2,1)S(1)} %bitcast.10) | data formatting | bytes 12582912
  85.1 0.0 collective-permute-done.10
  85.1 1.1 %concatenate.17 = bf16[192,768]{1,0:T(8,128)(2,1)S(1)} concatenate(bf16[12,768]{1,0:T(8,128)(2,1)S(1)} %collective-permute-done.10, bf16[12,768]{1,0:T(8,128)(2,1)S(1)} %collective-permute-done.9, bf16[12,768]{1,0:T(8,128)(2,1)S(1)} %collective-permute-done.8, bf16[12,768]{1,0:T(8,128)(2,1)S(1)} %collective-permute-done.7, bf16[12,768]{1,0:T(8,128)(2,1)S(1)} %collective-permute-done.6, ...), dimensions={0} | concatenate | bytes 589824 | tf_op jit(solution)/shard_map/jit(_roll_dynamic)/concatenate | solution.py:51
  86.2 4.9 %fusion.5 = f32[1,12,96,256]{3,2,1,0:T(8,128)} fusion(bf16[16,256,768]{2,1,0:T(8,128)(2,1)} %bitcast.11, bf16[192,768]{1,0:T(8,128)(2,1)S(1)} %concatenate.17, s32[]{:T(128)S(6)} %select_n.14), kind=kOutput, calls=%fused_computation.3 | convolution fusion | flops 453279744 | bytes 6045700 | tf_op jit(solution)/shard_map/amu,ju->ajm/dot_general | solution.py:55
  (7 shorter events, 0.0 us)
Async XLA Ops:
  0.8 10.8 %collective-permute-start = (bf16[12,32]{1,0:T(8,128)(2,1)S(1)}, bf16[12,32]{1,0:T(8,128)(2,1)S(1)}, u32[]{:S(2)}, u32[]{:S(2)}) collective-permute-start(bf16[12,32]{1,0:T(8,128)(2,1)S(1)} %get-tuple-element.72), channel_id=1, source_target_pairs={{0,1},{1,2},{2,3},{4,5},{5,6},{6,7},{8,9},{9,10},{10,11},{12,13},{... | collective-permute-start | bytes 2312 | tf_op jit(solution)/shard_map/ppermute | solution.py:16
  3.1 8.4 %collective-permute-start.1 = (bf16[12,32]{1,0:T(8,128)(2,1)S(1)}, bf16[12,32]{1,0:T(8,128)(2,1)S(1)}, u32[]{:S(2)}, u32[]{:S(2)}) collective-permute-start(bf16[12,32]{1,0:T(8,128)(2,1)S(1)} %get-tuple-element.73), channel_id=1, source_target_pairs={{1,0},{2,1},{3,2},{5,4},{6,5},{7,6},{9,8},{10,9},{11,10},{13,12},{... | collective-permute-start | bytes 2312 | tf_op jit(solution)/shard_map/ppermute | solution.py:19
  13.2 6.4 %collective-permute-start.2 = (bf16[12,128]{1,0:T(8,128)(2,1)S(1)}, bf16[12,128]{1,0:T(8,128)(2,1)S(1)}, u32[]{:S(2)}, u32[]{:S(2)}) collective-permute-start(bf16[12,128]{1,0:T(8,128)(2,1)S(1)} %get-tuple-element.70), channel_id=1, source_target_pairs={{0,1},{1,2},{2,3},{4,5},{5,6},{6,7},{8,9},{9,10},{10,11},{12,13},{... | collective-permute-start | bytes 9224 | tf_op jit(solution)/shard_map/ppermute | solution.py:16
  18.3 4.3 %collective-permute-start.3 = (bf16[12,128]{1,0:T(8,128)(2,1)S(1)}, bf16[12,128]{1,0:T(8,128)(2,1)S(1)}, u32[]{:S(2)}, u32[]{:S(2)}) collective-permute-start(bf16[12,128]{1,0:T(8,128)(2,1)S(1)} %get-tuple-element.71), channel_id=1, source_target_pairs={{1,0},{2,1},{3,2},{5,4},{6,5},{7,6},{9,8},{10,9},{11,10},{13,12},{... | collective-permute-start | bytes 9224 | tf_op jit(solution)/shard_map/ppermute | solution.py:19
  22.6 6.5 %collective-permute-start.4 = (bf16[12,768]{1,0:T(8,128)(2,1)S(1)}, bf16[12,768]{1,0:T(8,128)(2,1)S(1)}, u32[]{:S(2)}, u32[]{:S(2)}) collective-permute-start(bf16[12,768]{1,0:T(8,128)(2,1)S(1)} %pad_maximum_fusion), channel_id=1, source_target_pairs={{0,4},{4,8},{8,12},{12,16},{16,20},{20,24},{24,28},{28,0},{1,5},{5... | collective-permute-start | bytes 55304 | tf_op jit(solution)/shard_map/ppermute | solution.py:50
  29.1 6.5 %collective-permute-start.5 = (bf16[12,768]{1,0:T(8,128)(2,1)S(1)}, bf16[12,768]{1,0:T(8,128)(2,1)S(1)}, u32[]{:S(2)}, u32[]{:S(2)}) collective-permute-start(bf16[12,768]{1,0:T(8,128)(2,1)S(1)} %collective-permute-done.4), channel_id=1, source_target_pairs={{0,4},{4,8},{8,12},{12,16},{16,20},{20,24},{24,28},{28,0},{1,5},{5... | collective-permute-start | bytes 55304 | tf_op jit(solution)/shard_map/ppermute | solution.py:50
  35.7 6.5 %collective-permute-start.6 = (bf16[12,768]{1,0:T(8,128)(2,1)S(1)}, bf16[12,768]{1,0:T(8,128)(2,1)S(1)}, u32[]{:S(2)}, u32[]{:S(2)}) collective-permute-start(bf16[12,768]{1,0:T(8,128)(2,1)S(1)} %collective-permute-done.5), channel_id=1, source_target_pairs={{0,4},{4,8},{8,12},{12,16},{16,20},{20,24},{24,28},{28,0},{1,5},{5... | collective-permute-start | bytes 55304 | tf_op jit(solution)/shard_map/ppermute | solution.py:50
  42.2 6.5 %collective-permute-start.7 = (bf16[12,768]{1,0:T(8,128)(2,1)S(1)}, bf16[12,768]{1,0:T(8,128)(2,1)S(1)}, u32[]{:S(2)}, u32[]{:S(2)}) collective-permute-start(bf16[12,768]{1,0:T(8,128)(2,1)S(1)} %collective-permute-done.6), channel_id=1, source_target_pairs={{0,4},{4,8},{8,12},{12,16},{16,20},{20,24},{24,28},{28,0},{1,5},{5... | collective-permute-start | bytes 55304 | tf_op jit(solution)/shard_map/ppermute | solution.py:50
  48.7 6.5 %collective-permute-start.8 = (bf16[12,768]{1,0:T(8,128)(2,1)S(1)}, bf16[12,768]{1,0:T(8,128)(2,1)S(1)}, u32[]{:S(2)}, u32[]{:S(2)}) collective-permute-start(bf16[12,768]{1,0:T(8,128)(2,1)S(1)} %collective-permute-done.7), channel_id=1, source_target_pairs={{0,4},{4,8},{8,12},{12,16},{16,20},{20,24},{24,28},{28,0},{1,5},{5... | collective-permute-start | bytes 55304 | tf_op jit(solution)/shard_map/ppermute | solution.py:50
  55.2 6.5 %collective-permute-start.9 = (bf16[12,768]{1,0:T(8,128)(2,1)S(1)}, bf16[12,768]{1,0:T(8,128)(2,1)S(1)}, u32[]{:S(2)}, u32[]{:S(2)}) collective-permute-start(bf16[12,768]{1,0:T(8,128)(2,1)S(1)} %collective-permute-done.8), channel_id=1, source_target_pairs={{0,4},{4,8},{8,12},{12,16},{16,20},{20,24},{24,28},{28,0},{1,5},{5... | collective-permute-start | bytes 55304 | tf_op jit(solution)/shard_map/ppermute | solution.py:50
  61.8 23.3 %collective-permute-start.10 = (bf16[12,768]{1,0:T(8,128)(2,1)S(1)}, bf16[12,768]{1,0:T(8,128)(2,1)S(1)}, u32[]{:S(2)}, u32[]{:S(2)}) collective-permute-start(bf16[12,768]{1,0:T(8,128)(2,1)S(1)} %collective-permute-done.9), channel_id=1, source_target_pairs={{0,4},{4,8},{8,12},{12,16},{16,20},{20,24},{24,28},{28,0},{1,5},{5... | collective-permute-start | bytes 55304 | tf_op jit(solution)/shard_map/ppermute | solution.py:50
  78.2 2.8 %slice-start = ((bf16[12,196864]{1,0:T(8,128)(2,1)}), bf16[12,196608]{1,0:T(8,128)(2,1)S(1)}, s32[]{:S(2)}) async-start(bf16[12,196864]{1,0:T(8,128)(2,1)} %tile.10), calls=%async_computation | async-start | bytes 12582912 | tf_op jit(solution)/shard_map/slice | solution.py:45
